TPU v7x, 32 devices: a whole 2x2x4 slice. The times are simulated.
32 devices in a mesh: chan: 8 (over z, x), row: 4 (over y, core).
Axes of the slice: x: 2, y: 2, z: 4, core: 2. Of those that a mesh axis runs over, the one named last changes fastest.
Arguments:
- generator: float32 [8, 2048, 2048], P('chan', 'row'), may hold values from -0.125 to 0.125
- hamiltonian: float32 [8, 2048, 2048], P('chan', 'row'), may hold values from -6 to 6
- pp_width: int32 [8], P('chan'), may hold values from 1025 to 2048
- pp_orbit: int32 [8, 2, 2048], P('chan'), may hold values from 0 to 239
- ph_width: int32 [32], P(('chan', 'row')), may hold values from 513 to 1024
- ph_orbit: int32 [32, 2, 1024], P(('chan', 'row')), may hold values from 0 to 239
- occupation: int32 [240], replicated, may hold values 0 or 1
- send_tile: int32 [32, 32, 4], P(('chan', 'row')), may hold values from 0 to 63, as said below
- ph_source: int32 [32, 64, 2], P(('chan', 'row')), may hold values from 0 to 127, as said below
- ph_coef: float32 [32, 64, 2], P(('chan', 'row')), may hold values from -1.5 to 1.5
Outputs:
- commutator: float32 [8, 2048, 2048], P('chan', 'row')
Inputs may be any that keep to these rules, and one draw needn't show every extreme that they name: `send_tile`: every entry is a source tile number of device s; every slot carries a tile. ph_source[d] names every slot s * 4 + e exactly once.
All inputs are finite; a program needn't handle non-finite values.
Results may differ from a plain program's by a relative error of at most 0.0049.
Values may be sent and summed in bfloat16 or wider, within the bound.
A program may use at most 128 MiB of HBM per device.

v0:
```python
import jax
import jax.numpy as jnp
from jax import lax
from jax.sharding import PartitionSpec as P

TILE = 128


def occupancy(orbits, occupied):
    labels = jnp.arange(occupied.shape[0], dtype=jnp.int32)
    onehot = (orbits[:, :, None] == labels[None, None, :]).astype(jnp.float32)
    return jnp.einsum("ank,k->an", onehot, occupied, precision=lax.Precision.HIGHEST)


def to_tiles(block, tile_size):
    rows_count, cols_count = block.shape
    shaped = block.reshape(rows_count // tile_size, tile_size, cols_count // tile_size, tile_size)
    return shaped.transpose(0, 2, 1, 3).reshape(-1, tile_size, tile_size)


def from_tiles(tiles, rows_count, cols_count, tile_size):
    shaped = tiles.reshape(rows_count // tile_size, cols_count // tile_size, tile_size, tile_size)
    return shaped.transpose(0, 2, 1, 3).reshape(rows_count, cols_count)


def send_forward(outgoing):
    return (
        lax.all_to_all(outgoing[0], ("chan", "row"), split_axis=0, concat_axis=0, tiled=True),
        lax.all_to_all(outgoing[1], ("chan", "row"), split_axis=0, concat_axis=0, tiled=True),
    )


def send_back(returning):
    return lax.all_to_all(returning, ("chan", "row"), split_axis=0, concat_axis=0, tiled=True)


def on_device(
    generator,
    hamiltonian,
    pp_width,
    pp_orbit,
    ph_width,
    ph_orbit,
    occupation,
    send_tile,
    ph_source,
    ph_coef,
):
    slab_rows = generator.shape[1]
    full_width = generator.shape[2]
    hole_width = ph_orbit.shape[2]
    tile_size = TILE
    row_index = lax.axis_index("row")
    occupied = occupation.astype(jnp.float32)
    col_ok = jnp.arange(full_width, dtype=jnp.int32) < pp_width[0]
    row_ok = row_index * slab_rows + jnp.arange(slab_rows, dtype=jnp.int32) < pp_width[0]
    inside = row_ok[:, None] & col_ok[None, :]
    gen_b = jnp.where(inside, generator[0], 0.0).astype(jnp.bfloat16)
    ham_b = jnp.where(inside, hamiltonian[0], 0.0).astype(jnp.bfloat16)
    pair_occ = occupancy(pp_orbit[0], occupied)
    weight_pp = jnp.where(col_ok, 1.0 - pair_occ[0] - pair_occ[1], 0.0).astype(jnp.bfloat16)
    ham_piece = lax.all_gather(ham_b, "row", axis=0, tiled=True)
    gen_piece = lax.all_gather(gen_b, "row", axis=0, tiled=True)
    left_gen = gen_b * weight_pp[None, :]
    left_ham = ham_b * weight_pp[None, :]
    first = jnp.dot(left_gen, ham_piece, preferred_element_type=jnp.float32)
    second = jnp.dot(left_ham, gen_piece, preferred_element_type=jnp.float32)
    gen_tiles = to_tiles(gen_b, tile_size)
    ham_tiles = to_tiles(ham_b, tile_size)
    slot_tiles = send_tile[0]
    picked = jnp.maximum(slot_tiles, 0)
    got_gen, got_ham = send_forward((gen_tiles[picked], ham_tiles[picked]))
    references = ph_source[0]
    coefficients = ph_coef[0]

    def assemble(received):
        flat_tiles = received.reshape(-1, tile_size, tile_size)
        chosen = flat_tiles[references].astype(jnp.float32)
        summed = jnp.sum(coefficients[:, :, None, None] * chosen, axis=1).astype(jnp.bfloat16)
        return from_tiles(summed, hole_width, hole_width, tile_size)

    ph_gen = assemble(got_gen)
    ph_ham = assemble(got_ham)
    hole_cols = jnp.arange(hole_width, dtype=jnp.int32) < ph_width[0]
    hole_occ = occupancy(ph_orbit[0], occupied)
    weight_ph = jnp.where(hole_cols, hole_occ[0] - hole_occ[1], 0.0).astype(jnp.bfloat16)
    ph_comm = jnp.dot(ph_gen * weight_ph[None, :], ph_ham, preferred_element_type=jnp.float32)
    ph_comm = ph_comm - jnp.dot(
        ph_ham * weight_ph[None, :], ph_gen, preferred_element_type=jnp.float32
    )
    ph_comm = jnp.where(hole_cols[:, None] & hole_cols[None, :], ph_comm, 0.0).astype(jnp.bfloat16)
    comm_tiles = to_tiles(ph_comm, tile_size).astype(jnp.float32)
    weighted = coefficients[:, :, None, None] * comm_tiles[:, None]
    slot_total = got_gen.shape[0] * got_gen.shape[1]
    returned = jnp.zeros((slot_total, tile_size, tile_size), jnp.float32)
    returned = returned.at[references.reshape(-1)].add(weighted.reshape(-1, tile_size, tile_size))
    returned = returned.astype(jnp.bfloat16).reshape(got_gen.shape)
    arrived = send_back(returned)
    tile_total = gen_tiles.shape[0]
    target = jnp.where(slot_tiles >= 0, slot_tiles, tile_total).reshape(-1)
    collected = jnp.zeros((tile_total + 1, tile_size, tile_size), jnp.float32)
    collected = collected.at[target].add(
        arrived.reshape(-1, tile_size, tile_size).astype(jnp.float32)
    )[:-1]
    back_block = from_tiles(collected, slab_rows, full_width, tile_size)
    result = jnp.where(inside, first - second + back_block, 0.0)
    return result[None]


def solution(mesh):
    in_specs = (
        P("chan", "row", None),
        P("chan", "row", None),
        P("chan"),
        P("chan", None, None),
        P(("chan", "row")),
        P(("chan", "row"), None, None),
        P(),
        P(("chan", "row"), None, None),
        P(("chan", "row"), None, None),
        P(("chan", "row"), None, None),
    )
    out_specs = P("chan", "row", None)
    return jax.shard_map(
        on_device, mesh=mesh, in_specs=in_specs, out_specs=out_specs, check_vma=False
    )
```

profile of v0, /device:TPU:0, one launch (start us, length us, event | category | flops | bytes accessed | tf_op | source)
XLA Modules:
  0.0 458.0 jit_solution(822117082172704794)
XLA Ops:
  7.2 3.3 copy.41
  12.9 4.2 fusion.9
  18.1 3.0 gather_fusion
  21.1 7.5 %all-to-all-start = ((bf16[32,4,128,128]{3,2,1,0:T(8,128)(2,1)}), bf16[32,4,128,128]{3,2,1,0:T(8,128)(2,1)}, u32[]{:S(2)}, u32[]{:S(2)}) async-start(bf16[32,4,128,128]{3,2,1,0:T(8,128)(2,1)} %bitcast.130), calls=%async_computation | async-start | bytes 8388608 | tf_op jit(solution)/shard_map/all_to_all | solution.py:28
  28.6 7.0 %fusion.4 = (bf16[512,2048]{1,0:T(8,128)(2,1)}, bf16[512,2048]{1,0:T(8,128)(2,1)}) fusion(f32[1,512,2048]{2,1,0:T(8,128)} %param.10, pred[2048]{0:T(1024)(128)(4,1)S(1)} %iota_compare_fusion.4, pred[512]{0:T(512)(128)(4,1)S(1)} %add_compare_fusion.2, f32[1,512,2048]{2,1,0:T(8,128)} %param.11), kind=kLoop, calls=%fused_computation.18 | loop fusion | flops 3145728 | bytes 12585472 | tf_op jit(solution)/shard_map/convert_element_type | solution.py:58
  37.8 3.1 gather_fusion.2
  40.9 81.9 %all-to-all-done = bf16[32,4,128,128]{3,2,1,0:T(8,128)(2,1)} async-done(((bf16[32,4,128,128]{3,2,1,0:T(8,128)(2,1)}), bf16[32,4,128,128]{3,2,1,0:T(8,128)(2,1)}, u32[]{:S(2)}, u32[]{:S(2)}) %all-to-all-start) | async-done | bytes 4194336 | tf_op jit(solution)/shard_map/all_to_all | solution.py:28
  122.9 5.1 %all-to-all-start.1 = ((bf16[32,4,128,128]{3,2,1,0:T(8,128)(2,1)}), bf16[32,4,128,128]{3,2,1,0:T(8,128)(2,1)}, u32[]{:S(2)}, u32[]{:S(2)}) async-start(bf16[32,4,128,128]{3,2,1,0:T(8,128)(2,1)} %bitcast.129), calls=%async_computation.1 | async-start | bytes 8388608 | tf_op jit(solution)/shard_map/all_to_all | solution.py:29
  131.6 5.2 %gather_fusion.1 = bf16[128,128,128]{2,1,0:T(8,128)(2,1)} fusion(bf16[128,128,128]{2,1,0:T(8,128)(2,1)} %bitcast.13, s32[1024]{0:T(1024)S(1)} %pad_clamp_fusion), kind=kCustom, calls=%fused_computation.1 | custom fusion | bytes 8389120 | tf_op jit(solution)/shard_map/gather | solution.py:78
  136.9 85.4 %all-to-all-done.1 = bf16[32,4,128,128]{3,2,1,0:T(8,128)(2,1)} async-done(((bf16[32,4,128,128]{3,2,1,0:T(8,128)(2,1)}), bf16[32,4,128,128]{3,2,1,0:T(8,128)(2,1)}, u32[]{:S(2)}, u32[]{:S(2)}) %all-to-all-start.1) | async-done | bytes 4194336 | tf_op jit(solution)/shard_map/all_to_all | solution.py:29
  222.3 5.3 %gather_fusion.3 = bf16[128,128,128]{2,1,0:T(8,128)(2,1)} fusion(bf16[128,128,128]{2,1,0:T(8,128)(2,1)} %bitcast.24, s32[1024]{0:T(1024)S(1)} %pad_clamp_fusion), kind=kCustom, calls=%fused_computation.3 | custom fusion | bytes 8389120 | tf_op jit(solution)/shard_map/gather | solution.py:78
  227.6 6.9 %fusion = (bf16[64,128,128]{2,1,0:T(8,128)(2,1)S(1)}, bf16[64,128,128]{2,1,0:T(8,128)(2,1)S(1)}) fusion(f32[64,2]{1,0:T(8,128)S(1)} %copy.28, bf16[128,128,128]{2,1,0:T(8,128)(2,1)} %gather_fusion.3, bf16[128,128,128]{2,1,0:T(8,128)(2,1)} %gather_fusion.1), kind=kLoop, calls=%fused_computation.7 | loop fusion | flops 10485760 | bytes 12583424 | tf_op jit(solution)/shard_map/reduce_sum | solution.py:79
  246.7 13.0 %bitcast_multiply_fusion = f32[128,128,128]{2,1,0:T(8,128)} fusion(f32[64,128,128]{2,1,0:T(8,128)S(1)} %bitcast.131, f32[128]{0:T(128)S(1)} %mul.80), kind=kLoop, calls=%fused_computation.10 | loop fusion | flops 2097152 | bytes 12583424 | tf_op jit(solution)/shard_map/mul | solution.py:93
  259.7 4.3 broadcast_in_dim.54
  264.0 26.7 %scatter_fusion = f32[128,128,128]{2,1,0:T(8,128)} fusion(f32[128,128,128]{2,1,0:T(8,128)} %broadcast_in_dim.54, s32[128]{0:T(128)S(1)} %fusion.37, f32[128,128,128]{2,1,0:T(8,128)} %bitcast_multiply_fusion), kind=kCustom, calls=%fused_computation.4 | custom fusion | flops 2097152 | bytes 25166336 | tf_op jit(solution)/shard_map/scatter-add | solution.py:96
  290.7 6.4 %convert_element_type.91 = bf16[128,128,128]{2,1,0:T(8,128)(2,1)} convert(f32[128,128,128]{2,1,0:T(8,128)} %scatter_fusion) | non-fusion elementwise | flops 2097152 | bytes 12582912 | tf_op jit(solution)/shard_map/convert_element_type | solution.py:97
  297.1 5.1 %all-to-all-start.2 = ((bf16[32,4,128,128]{3,2,1,0:T(8,128)(2,1)}), bf16[32,4,128,128]{3,2,1,0:T(8,128)(2,1)}, u32[]{:S(2)}, u32[]{:S(2)}) async-start(bf16[32,4,128,128]{3,2,1,0:T(8,128)(2,1)} %bitcast.128), calls=%async_computation.2 | async-start | bytes 8388608 | tf_op jit(solution)/shard_map/all_to_all | solution.py:34
  304.8 9.4 %fusion.21 = f32[512,2048]{1,0:T(8,128)} fusion(bf16[2048,2048]{1,0:T(8,128)(2,1)} %all-gather.3.cloned.1.call-done, bf16[512,2048]{1,0:T(8,128)(2,1)S(1)} %copy-done.2, bf16[2048]{0:T(1024)(128)(2,1)S(1)} %fusion.33), kind=kOutput, calls=%fused_computation.41 | convolution fusion | flops 4296015872 | bytes 14684160 | tf_op jit(solution)/shard_map/dot_general | solution.py:66
  314.2 82.3 %all-to-all-done.2 = bf16[32,4,128,128]{3,2,1,0:T(8,128)(2,1)} async-done(((bf16[32,4,128,128]{3,2,1,0:T(8,128)(2,1)}), bf16[32,4,128,128]{3,2,1,0:T(8,128)(2,1)}, u32[]{:S(2)}, u32[]{:S(2)}) %all-to-all-start.2) | async-done | bytes 4194336 | tf_op jit(solution)/shard_map/all_to_all | solution.py:34
  396.5 6.5 %bitcast_convert_fusion = f32[128,128,128]{2,1,0:T(8,128)} fusion(bf16[32,4,128,128]{3,2,1,0:T(8,128)(2,1)} %all-to-all-done.2), kind=kLoop, calls=%fused_computation.22 | loop fusion | flops 2097152 | bytes 12582912 | tf_op jit(solution)/shard_map/convert_element_type | solution.py:103
  403.0 2.5 broadcast_in_dim.52
  405.5 26.6 %scatter_fusion.1 = f32[65,128,128]{2,1,0:T(8,128)} fusion(f32[65,128,128]{2,1,0:T(8,128)} %broadcast_in_dim.52, s32[128]{0:T(128)S(1)} %fusion.36, f32[128,128,128]{2,1,0:T(8,128)} %bitcast_convert_fusion), kind=kCustom, calls=%fused_computation.5 | custom fusion | flops 2097152 | bytes 25166336 | tf_op jit(solution)/shard_map/scatter-add | solution.py:102
  434.5 4.4 copy.38
  438.9 12.0 %fusion.6 = f32[1,512,2048]{2,1,0:T(8,128)} fusion(f32[64,8,16,128]{3,2,1,0:T(8,128)} %bitcast.138, f32[512,2048]{1,0:T(8,128)} %fusion.21, bf16[2048,2048]{1,0:T(8,128)(2,1)} %all-gather.5.cloned.1.call-done, bf16[512,2048]{1,0:T(8,128)(2,1)S(1)} %copy-done.1, pred[2048]{0:T(1024)(128)(4,1)S(1)} %iota_compare_fusion.4, ...), kind=kOutput, calls=%fused_computation.20 | convolution fusion | flops 4300210176 | bytes 23075328 | tf_op jit(solution)/shard_map/dot_general | solution.py:67
  (66 shorter events, 25.6 us)
Async XLA Ops:
  7.2 3.5 copy-start
  17.2 0.7 copy-start.3
  21.1 101.7 %all-to-all-start = ((bf16[32,4,128,128]{3,2,1,0:T(8,128)(2,1)}), bf16[32,4,128,128]{3,2,1,0:T(8,128)(2,1)}, u32[]{:S(2)}, u32[]{:S(2)}) async-start(bf16[32,4,128,128]{3,2,1,0:T(8,128)(2,1)} %bitcast.130), calls=%async_computation | async-start | bytes 8388608 | tf_op jit(solution)/shard_map/all_to_all | solution.py:28
  28.6 276.2 %all-gather.3.cloned.1.call-start = ((), (), s32[]{:S(2)}) async-start(), calls=%async_computation.3 | async-start | bytes 10485760 | tf_op jit(solution)/shard_map/all_gather | solution.py:62
  122.8 5.9 %copy-start.5 = (s32[1,64,2]{1,2,0:T(2,128)S(1)}, s32[1,64,2]{1,2,0:T(2,128)}, u32[]{:S(2)}) copy-start(s32[1,64,2]{1,2,0:T(2,128)} %param.18) | copy-start | bytes 1540
  122.8 6.3 %copy-start.4 = (f32[1,64,2]{1,2,0:T(2,128)S(1)}, f32[1,64,2]{1,2,0:T(2,128)}, u32[]{:S(2)}) copy-start(f32[1,64,2]{1,2,0:T(2,128)} %param.19) | copy-start | bytes 1540
  122.9 6.5 %copy-start.6 = (s32[240]{0:T(256)S(1)}, s32[240]{0:T(256)}, u32[]{:S(2)}) copy-start(s32[240]{0:T(256)} %param.16) | copy-start | bytes 2884
  122.9 6.5 %copy-start.8 = (s32[1,2,1024]{2,1,0:T(2,128)S(1)}, s32[1,2,1024]{2,1,0:T(2,128)}, u32[]{:S(2)}) copy-start(s32[1,2,1024]{2,1,0:T(2,128)} %param.15) | copy-start | bytes 24580
  122.9 99.4 %all-to-all-start.1 = ((bf16[32,4,128,128]{3,2,1,0:T(8,128)(2,1)}), bf16[32,4,128,128]{3,2,1,0:T(8,128)(2,1)}, u32[]{:S(2)}, u32[]{:S(2)}) async-start(bf16[32,4,128,128]{3,2,1,0:T(8,128)(2,1)} %bitcast.129), calls=%async_computation.1 | async-start | bytes 8388608 | tf_op jit(solution)/shard_map/all_to_all | solution.py:29
  128.0 310.9 %all-gather.5.cloned.1.call-start = ((), (), s32[]{:S(2)}) async-start(), calls=%async_computation.4 | async-start | bytes 10485760 | tf_op jit(solution)/shard_map/all_gather | solution.py:63
  297.1 5.4 %copy-start.7 = (s32[1,2,2048]{2,1,0:T(2,128)S(1)}, s32[1,2,2048]{2,1,0:T(2,128)}, u32[]{:S(2)}) copy-start(s32[1,2,2048]{2,1,0:T(2,128)} %param.13) | copy-start | bytes 49156
  297.1 7.7 %copy-start.2 = (bf16[512,2048]{1,0:T(8,128)(2,1)S(1)}, bf16[512,2048]{1,0:T(8,128)(2,1)}, u32[]{:S(2)}) copy-start(bf16[512,2048]{1,0:T(8,128)(2,1)} %get-tuple-element.7) | copy-start | bytes 6291460
  297.1 99.4 %all-to-all-start.2 = ((bf16[32,4,128,128]{3,2,1,0:T(8,128)(2,1)}), bf16[32,4,128,128]{3,2,1,0:T(8,128)(2,1)}, u32[]{:S(2)}, u32[]{:S(2)}) async-start(bf16[32,4,128,128]{3,2,1,0:T(8,128)(2,1)} %bitcast.128), calls=%async_computation.2 | async-start | bytes 8388608 | tf_op jit(solution)/shard_map/all_to_all | solution.py:34
  434.5 4.4 copy-start.1
Sparse Core Ops, SparseCore 0:
  35.8 87.3 all-gather.2
  130.4 92.2 all-gather.4
where the time goes:
time: 463 us; the launch traced here: 458 us
  waiting for transfers between devices  250 us (54%)
  other arithmetic  97.7 us (21%)
  local copies, waits for them, and re-layouts  47.3 us (10%)
  matrix products  29.6 us (6%)
  starting transfers between devices  17.8 us (4%)
  between operations  15.2 us (3%)
    all_to_all x1, waiting for transfers between devices, send_forward(): lax.all_to_all(outgoing[1], ('chan', 'row'), split_axis=0, concat_axis=0,...  85.4 us
    all_to_all x1, waiting for transfers between devices, send_back(): lax.all_to_all(returning, ('chan', 'row'), split_axis=0, concat_axis=0, t...  82.3 us
    all_to_all x1, waiting for transfers between devices, send_forward(): lax.all_to_all(outgoing[0], ('chan', 'row'), split_axis=0, concat_axis=0,...  81.9 us
    scatter-add x1, other arithmetic, on_device(): returned.at[references.reshape(-1)]  26.7 us
    scatter-add x1, other arithmetic, on_device(): collected.at[target]  26.6 us
    mul x1, other arithmetic, on_device(): weighted = coefficients[:, :, None, None] * comm_tiles[:, None]  13 us
    dot_general x1, matrix products, on_device(): second = jnp.dot(left_ham, gen_piece, preferred_element_type=jnp.float32)  12 us
    gather x2, local copies, waits for them, and re-layouts, assemble(): chosen = flat_tiles[references].astype(jnp.float32)  10.5 us
  transfers between devices with their start and end apart: 5, of which 3 were waited for; matrix products, arithmetic and copies ran while one was open for 32% of the time, Pallas kernels for 0%

commit v1 on v0

v1 whole, which is shorter than its diff:
```python
import functools

import jax
import jax.numpy as jnp
from jax import lax
from jax.experimental import pallas as pl
from jax.experimental.pallas import tpu as pltpu
from jax.sharding import PartitionSpec as P

TILE = 128
F32 = jnp.float32
BF16 = jnp.bfloat16


def params(limit=60 << 20):
    return pltpu.CompilerParams(vmem_limit_bytes=limit)


def cost(moved, flops=0):
    return pl.CostEstimate(flops=flops, bytes_accessed=moved, transcendentals=0)


def select_kernel(row_tiles, step_slots, cap, idx, width, rows_left, x_ref, b_ref, out_ref, tiles):
    i = pl.program_id(0)

    @pl.when(i < row_tiles)
    def _():
        x = x_ref[...]
        rows = i * TILE + lax.broadcasted_iota(jnp.int32, x.shape, 0)
        cols = lax.broadcasted_iota(jnp.int32, x.shape, 1)
        v = jnp.where((rows < rows_left[0]) & (cols < width[0]), x, 0.0).astype(BF16)
        b_ref[...] = v
        col_tiles = x.shape[1] // TILE
        for c in range(col_tiles):
            tiles[i * col_tiles + c] = v[:, c * TILE : (c + 1) * TILE]

    @pl.when(i >= row_tiles)
    def _():
        first = (i - row_tiles) * step_slots
        for k in range(step_slots):
            s = first + k
            out_ref[k] = tiles[idx[s // cap, s % cap]]


def select_tiles(slab, width, rows_left, slots):
    rows, cols = slab.shape
    peers, cap = slots.shape
    total = peers * cap
    row_tiles = rows // TILE
    step_slots = 32
    return pl.pallas_call(
        functools.partial(select_kernel, row_tiles, step_slots, cap),
        grid_spec=pltpu.PrefetchScalarGridSpec(
            num_scalar_prefetch=3,
            grid=(row_tiles + total // step_slots,),
            in_specs=[pl.BlockSpec((TILE, cols), lambda i, *_: (jnp.minimum(i, row_tiles - 1), 0))],
            out_specs=(
                pl.BlockSpec((TILE, cols), lambda i, *_: (jnp.minimum(i, row_tiles - 1), 0)),
                pl.BlockSpec((step_slots, TILE, TILE), lambda i, *_: (jnp.maximum(i - row_tiles, 0), 0, 0)),
            ),
            scratch_shapes=[pltpu.VMEM((row_tiles * (cols // TILE), TILE, TILE), BF16)],
        ),
        out_shape=(
            jax.ShapeDtypeStruct((rows, cols), BF16),
            jax.ShapeDtypeStruct((total, TILE, TILE), BF16),
        ),
        compiler_params=params(),
        cost_estimate=cost(6 * rows * cols + 2 * total * TILE * TILE),
        name="select_tiles",
    )(slots, width, rows_left, slab)


def assemble_rows(i, side, src, coef, recv, dst, dst_w, w):
    for c in range(side):
        t = i * side + c
        one = recv[src[t, 0]].astype(F32) * coef[t, 0]
        two = recv[src[t, 1]].astype(F32) * coef[t, 1]
        tile = (one + two).astype(BF16)
        cols = slice(c * TILE, (c + 1) * TILE)
        rows = pl.ds(pl.multiple_of(i * TILE, TILE), TILE)
        dst[rows, cols] = tile
        dst_w[rows, cols] = tile * w[:, cols]


def assemble_kernel(side, src, coef, recv, w, g_ref, gw_ref):
    @pl.loop(0, side)
    def _(i):
        assemble_rows(i, side, src, coef, recv, g_ref, gw_ref, w)


def assemble(recv, src, coef, w):
    width = w.shape[1]
    smem = pl.BlockSpec(memory_space=pltpu.SMEM)
    vmem = pl.BlockSpec(memory_space=pltpu.VMEM)
    return pl.pallas_call(
        functools.partial(assemble_kernel, width // TILE),
        in_specs=[smem, smem, vmem, vmem],
        out_specs=(vmem, vmem),
        out_shape=(jax.ShapeDtypeStruct((width, width), BF16),) * 2,
        compiler_params=params(),
        cost_estimate=cost(2 * recv.size + 4 * width * width),
        name="assemble",
    )(src, coef, recv, w)


def commutator_kernel(side, src, coef, width, recv, w, g_ref, gw_ref, out_ref, h, hw, comm):
    @pl.loop(0, side)
    def _(i):
        assemble_rows(i, side, src, coef, recv, h, hw, w)

    full = side * TILE
    step = 2 * TILE

    @pl.loop(0, full // step)
    def _(j):
        cols = pl.ds(pl.multiple_of(j * step, step), step)
        c = jnp.dot(gw_ref[...], h[:, cols], preferred_element_type=F32)
        c = c - jnp.dot(hw[...], g_ref[:, cols], preferred_element_type=F32)
        row = lax.broadcasted_iota(jnp.int32, (full, step), 0)
        col = j * step + lax.broadcasted_iota(jnp.int32, (full, step), 1)
        comm[:, cols] = jnp.where((row < width[0]) & (col < width[0]), c, 0.0).astype(BF16)

    @pl.loop(0, side)
    def _(i):
        rows = pl.ds(pl.multiple_of(i * TILE, TILE), TILE)
        for c in range(side):
            t = i * side + c
            tile = comm[rows, c * TILE : (c + 1) * TILE].astype(F32)
            out_ref[src[t, 0]] = (tile * coef[t, 0]).astype(BF16)
            out_ref[src[t, 1]] = (tile * coef[t, 1]).astype(BF16)


def commutator(recv, src, coef, hole, w, g, gw):
    full = w.shape[1]
    smem = pl.BlockSpec(memory_space=pltpu.SMEM)
    vmem = pl.BlockSpec(memory_space=pltpu.VMEM)
    return pl.pallas_call(
        functools.partial(commutator_kernel, full // TILE),
        in_specs=[smem, smem, smem, vmem, vmem, vmem, vmem],
        out_specs=vmem,
        out_shape=jax.ShapeDtypeStruct(recv.shape, BF16),
        scratch_shapes=[pltpu.VMEM((full, full), BF16)] * 3,
        compiler_params=params(),
        cost_estimate=cost(4 * recv.size + 4 * full * full, 4 * full * full * full),
        name="commutator",
    )(src, coef, hole, recv, w, g, gw)


def finish_kernel(steps, step_slots, cap, col_tiles, idx, width, rows_left, arrived, direct, out_ref, acc):
    i = pl.program_id(0)

    @pl.when(i == 0)
    def _():
        acc[...] = direct[...]

    @pl.when(i < steps)
    def _():
        for k in range(step_slots):
            s = i * step_slots + k
            j = idx[s // cap, s % cap]
            rows = pl.ds(pl.multiple_of(j // col_tiles * TILE, TILE), TILE)
            cols = pl.ds(pl.multiple_of(j % col_tiles * TILE, TILE), TILE)
            acc[rows, cols] += arrived[k].astype(F32)

    @pl.when(i >= steps)
    def _():
        base = (i - steps) * TILE
        v = acc[pl.ds(pl.multiple_of(base, TILE), TILE), :]
        rows = base + lax.broadcasted_iota(jnp.int32, v.shape, 0)
        cols = lax.broadcasted_iota(jnp.int32, v.shape, 1)
        out_ref[...] = jnp.where((rows < rows_left[0]) & (cols < width[0]), v, 0.0)


def finish(arrived, direct, width, rows_left, slots):
    rows, cols = direct.shape
    peers, cap = slots.shape
    step_slots = 16
    steps = peers * cap // step_slots
    return pl.pallas_call(
        functools.partial(finish_kernel, steps, step_slots, cap, cols // TILE),
        grid_spec=pltpu.PrefetchScalarGridSpec(
            num_scalar_prefetch=3,
            grid=(steps + rows // TILE,),
            in_specs=[
                pl.BlockSpec((step_slots, TILE, TILE), lambda i, *_: (jnp.minimum(i, steps - 1), 0, 0)),
                pl.BlockSpec((rows, cols), lambda i, *_: (0, 0)),
            ],
            out_specs=pl.BlockSpec((TILE, cols), lambda i, *_: (jnp.maximum(i - steps, 0), 0)),
            scratch_shapes=[pltpu.VMEM((rows, cols), F32)],
        ),
        out_shape=jax.ShapeDtypeStruct((rows, cols), F32),
        compiler_params=params(),
        cost_estimate=cost(2 * arrived.size + 8 * rows * cols),
        name="finish",
    )(slots, width, rows_left, arrived, direct)


def occupancy(orbits, occupation):
    labels = jnp.arange(occupation.shape[0], dtype=jnp.int32)
    hit = (orbits[:, :, None] == labels) & (occupation == 1)
    return jnp.sum(hit.astype(F32), axis=2)


def exchange(tiles, peers):
    shaped = tiles.reshape((peers, -1) + tiles.shape[1:])
    moved = lax.all_to_all(shaped, ("chan", "row"), split_axis=0, concat_axis=0, tiled=True)
    return moved.reshape(tiles.shape)


def on_device(
    generator, hamiltonian, pp_width, pp_orbit, ph_width, ph_orbit, occupation, send_tile, ph_source, ph_coef
):
    slab_rows = generator.shape[1]
    full_width = generator.shape[2]
    hole_width = ph_orbit.shape[2]
    slots = send_tile[0]
    src = ph_source[0]
    coef = ph_coef[0]
    peers = slots.shape[0]
    rows_left = pp_width - lax.axis_index("row") * slab_rows

    gen_b, gen_out = select_tiles(generator[0], pp_width, rows_left, slots)
    got_gen = exchange(gen_out, peers)
    ham_in, gen_b = lax.optimization_barrier((hamiltonian[0], gen_b))
    ham_b, ham_out = select_tiles(ham_in, pp_width, rows_left, slots)
    got_ham = exchange(ham_out, peers)

    pp_orbit, ph_orbit, ham_b = lax.optimization_barrier((pp_orbit, ph_orbit, ham_b))
    col_ok = jnp.arange(full_width, dtype=jnp.int32) < pp_width[0]
    pair = occupancy(pp_orbit[0], occupation)
    weight_pp = jnp.where(col_ok, 1.0 - pair[0] - pair[1], 0.0).astype(BF16)
    hole_cols = jnp.arange(hole_width, dtype=jnp.int32) < ph_width[0]
    hole = occupancy(ph_orbit[0], occupation)
    weight_ph = jnp.where(hole_cols, hole[0] - hole[1], 0.0).astype(BF16)[None]

    gen_all = lax.all_gather(gen_b, "row", axis=0, tiled=True)
    ham_all = lax.all_gather(ham_b, "row", axis=0, tiled=True)
    first = jnp.dot(gen_b * weight_pp[None, :], ham_all, preferred_element_type=F32)
    second = jnp.dot(ham_b * weight_pp[None, :], gen_all, preferred_element_type=F32)
    direct = first - second

    ph_gen, ph_gen_w = assemble(got_gen, src, coef, weight_ph)
    returned = commutator(got_ham, src, coef, ph_width, weight_ph, ph_gen, ph_gen_w)
    arrived = exchange(returned, peers)
    return finish(arrived, direct, pp_width, rows_left, slots)[None]


def solution(mesh):
    in_specs = (
        P("chan", "row", None),
        P("chan", "row", None),
        P("chan"),
        P("chan", None, None),
        P(("chan", "row")),
        P(("chan", "row"), None, None),
        P(),
        P(("chan", "row"), None, None),
        P(("chan", "row"), None, None),
        P(("chan", "row"), None, None),
    )
    out_specs = P("chan", "row", None)
    return jax.shard_map(
        on_device, mesh=mesh, in_specs=in_specs, out_specs=out_specs, check_vma=False
    )
```

time: 463 us -> 354 us (0.76)
  blocking collectives: 0 us -> 101 us
  other arithmetic: 97.7 us -> 1.93 us
  waiting for transfers between devices: 250 us -> 158 us
  Pallas kernels: 0 us -> 44.8 us
  local copies, waits for them, and re-layouts: 47.3 us -> 2.79 us
  starting transfers between devices: 17.8 us -> 8.98 us
  matrix products: 29.6 us -> 21.1 us
    all_to_all x0 -> x1, blocking collectives: none -> 101 us  [exchange(): lax.all_to_all(shaped, ('chan', 'row'), split_axis=0, concat_axis=0, tile...]
    all_to_all x3 -> x2, waiting for transfers between devices: 250 us -> 157 us  [exchange(): lax.all_to_all(shaped, ('chan', 'row'), split_axis=0, concat_axis=0, tile...]
    scatter-add x2 -> x0, other arithmetic: 53.3 us -> none  [the longest x1 26.7 us: on_device(): returned.at[references.reshape(-1)]]
    pallas_call x0 -> x5, Pallas kernels: none -> 44.8 us  [the longest x2 15.7 us: select_tiles(): pl.pallas_call(functools.partial(select_kernel, row_tiles, step_slots, ca...]
    convert_element_type x6 -> x2, other arithmetic: 20 us -> 0.64 us  [the longest x1 0.6 us: on_device(): weight_ph = jnp.where(hole_cols, hole[0] - hole[1], 0.0).astype(BF16)[None]]
    gather x4 -> x0, local copies, waits for them, and re-layouts: 16.6 us -> none  [the longest x2 10.5 us: assemble(): chosen = flat_tiles[references].astype(jnp.float32)]
    mul x2 -> x0, other arithmetic: 13.2 us -> none  [the longest x1 13 us: on_device(): weighted = coefficients[:, :, None, None] * comm_tiles[:, None]]
    transpose x5 -> x0, local copies, waits for them, and re-layouts: 9.8 us -> none  [the longest x3 7.13 us: from_tiles(): return shaped.transpose(0, 2, 1, 3).reshape(rows_count, cols_count)]
  transfers between devices with their start and end apart: 5 -> 4, of which waited for: 3 -> 2; matrix products, arithmetic and copies ran while one was open for 32% -> 7% of each run, Pallas kernels for 0% -> 5%
where the time goes in v1:
time: 354 us; the launch traced here: 353 us
  waiting for transfers between devices  158 us (45%)
  blocking collectives  101 us (29%)
  Pallas kernels  44.8 us (13%)
  matrix products  21.1 us (6%)
  between operations  14.8 us (4%)
  starting transfers between devices  8.98 us (3%)
    all_to_all x2, waiting for transfers between devices, exchange(): lax.all_to_all(shaped, ('chan', 'row'), split_axis=0, concat_axis=0, tile...  157 us
    all_to_all x1, blocking collectives, exchange(): lax.all_to_all(shaped, ('chan', 'row'), split_axis=0, concat_axis=0, tile...  101 us
    pallas_call x2, Pallas kernels, select_tiles(): pl.pallas_call(functools.partial(select_kernel, row_tiles, step_slots, ca...  15.7 us
    pallas_call x1, Pallas kernels, commutator(): pl.pallas_call(functools.partial(commutator_kernel, full // TILE), in_spe...  12.8 us
    dot_general x1, matrix products, on_device(): jnp.dot(ham_b * weight_pp[None, :], gen_all, preferred_element_type=F32)  11.6 us
    pallas_call x1, Pallas kernels, finish(): pl.pallas_call(functools.partial(finish_kernel, steps, step_slots, cap, c...  10.7 us
    dot_general x1, matrix products, on_device(): jnp.dot(gen_b * weight_pp[None, :], ham_all, preferred_element_type=F32)  9.41 us
    all_to_all x2, starting transfers between devices, exchange(): lax.all_to_all(shaped, ('chan', 'row'), split_axis=0, concat_axis=0, tile...  8.93 us
  transfers between devices with their start and end apart: 4, of which 2 were waited for; matrix products, arithmetic and copies ran while one was open for 7% of the time, Pallas kernels for 5%

profile of v1, /device:TPU:0, one launch (start us, length us, event | category | flops | bytes accessed | tf_op | source)
XLA Modules:
  0.0 353.2 jit_solution(10709667755708799512)
XLA Ops:
  6.5 0.0 all-gather.3.cloned.1.call-start
  6.5 1.4 copy.24.idx
  8.6 7.8 %select_tiles.2 = (bf16[512,2048]{1,0:T(8,128)(2,1)}, bf16[128,128,128]{2,1,0:T(8,128)(2,1)}) custom-call(s32[32,4]{1,0:T(8,128)} %copy.24.idx, s32[1]{0:T(128)} %copy.25.width, s32[1]{0:T(128)S(6)} %sub.25.rows_left, f32[512,2048]{1,0:T(8,128)} %bitcast.22), custom_call_target="tpu_custom_call" | custom-call | bytes 10485760 | tf_op jit(solution)/shard_map/select_tiles/pallas_call | solution.py:51
  16.4 7.8 %select_tiles.3 = (bf16[512,2048]{1,0:T(8,128)(2,1)}, bf16[128,128,128]{2,1,0:T(8,128)(2,1)}) custom-call(s32[32,4]{1,0:T(8,128)} %copy.24.idx, s32[1]{0:T(128)} %copy.25.width, s32[1]{0:T(128)S(6)} %sub.25.rows_left, f32[512,2048]{1,0:T(8,128)} %bitcast.23), custom_call_target="tpu_custom_call" | custom-call | bytes 10485760 | tf_op jit(solution)/shard_map/select_tiles/pallas_call | solution.py:51
  24.2 0.0 all-gather.3.cloned.1.call-update
  24.2 101.1 %all_to_all.15 = bf16[32,4,128,128]{3,2,1,0:T(8,128)(2,1)} all-to-all(bf16[32,4,128,128]{3,2,1,0:T(8,128)(2,1)} %bitcast.26), channel_id=1, replica_groups=mesh['chan'=8,'row'=4] {'chan','row'}, dimensions={0} | all-to-all | bytes 8388608 | tf_op jit(solution)/shard_map/all_to_all | solution.py:206
  125.3 3.8 %all-to-all-start = ((bf16[32,4,128,128]{3,2,1,0:T(8,128)(2,1)}), bf16[32,4,128,128]{3,2,1,0:T(8,128)(2,1)}, u32[]{:S(2)}, u32[]{:S(2)}) async-start(bf16[32,4,128,128]{3,2,1,0:T(8,128)(2,1)} %bitcast.24), calls=%async_computation | async-start | bytes 8388608 | tf_op jit(solution)/shard_map/all_to_all | solution.py:206
  129.1 0.0 all-gather.5.cloned.1.call-start
  129.2 0.7 all-gather.5.cloned.1.call-update
  129.9 0.7 copy.22.src
  130.6 0.7 copy.23.coef
  132.0 0.0 copy-done.5
  132.0 0.4 convert_reduce_fusion.1
  132.4 0.6 fusion.9.w
  133.0 5.6 %assemble.1 = (bf16[1024,1024]{1,0:T(8,128)(2,1)}, bf16[1024,1024]{1,0:T(8,128)(2,1)}) custom-call(s32[64,2]{1,0:T(8,128)} %copy.22.src, f32[64,2]{1,0:T(8,128)} %copy.23.coef, bf16[128,128,128]{2,1,0:T(8,128)(2,1)} %bitcast.21, bf16[1,1024]{1,0:T(2,128)(2,1)} %fusion.9.w), custom_call_target="tpu_custom_call" | custom-call | bytes 8388608 | tf_op jit(solution)/shard_map/assemble/pallas_call | solution.py:95
  138.5 84.9 %all-to-all-done = bf16[32,4,128,128]{3,2,1,0:T(8,128)(2,1)} async-done(((bf16[32,4,128,128]{3,2,1,0:T(8,128)(2,1)}), bf16[32,4,128,128]{3,2,1,0:T(8,128)(2,1)}, u32[]{:S(2)}, u32[]{:S(2)}) %all-to-all-start) | async-done | bytes 4194336 | tf_op jit(solution)/shard_map/all_to_all | solution.py:206
  223.4 12.8 %commutator.1 = bf16[128,128,128]{2,1,0:T(8,128)(2,1)} custom-call(s32[64,2]{1,0:T(8,128)} %copy.22.src, f32[64,2]{1,0:T(8,128)} %copy.23.coef, s32[1]{0:T(128)} %copy.26.width, bf16[128,128,128]{2,1,0:T(8,128)(2,1)} %bitcast.7.recv, bf16[1,1024]{1,0:T(2,128)(2,1)} %fusion.9.w, bf16[1024,1024]{1,0:T(8,128)(2,1)} %get-tuple-element.22.g_ref, ...), custom_call_target="tpu_custom_call" | custom-call | flops 4294967296 | bytes 12582912 | tf_op jit(solution)/shard_map/commutator/pallas_call | solution.py:137
  236.3 5.1 %all-to-all-start.2 = ((bf16[32,4,128,128]{3,2,1,0:T(8,128)(2,1)}), bf16[32,4,128,128]{3,2,1,0:T(8,128)(2,1)}, u32[]{:S(2)}, u32[]{:S(2)}) async-start(bf16[32,4,128,128]{3,2,1,0:T(8,128)(2,1)} %bitcast.25), calls=%async_computation.2 | async-start | bytes 8388608 | tf_op jit(solution)/shard_map/all_to_all | solution.py:206
  241.4 0.9 convert_reduce_fusion
  242.4 0.0 all-gather.3.cloned.1.call-done
  242.4 9.4 %fusion.2 = f32[512,2048]{1,0:T(8,128)} fusion(bf16[2048,2048]{1,0:T(8,128)(2,1)} %all-gather.3.cloned.1.call-done, bf16[512,2048]{1,0:T(8,128)(2,1)S(1)} %copy-done, bf16[2048]{0:T(1024)(128)(2,1)S(1)} %fusion.8), kind=kOutput, calls=%fused_computation.5 | convolution fusion | flops 4296015872 | bytes 14684160 | tf_op jit(solution)/shard_map/dot_general | solution.py:238
  251.8 11.6 %convolution_subtract_fusion.direct = f32[512,2048]{1,0:T(8,128)} fusion(f32[512,2048]{1,0:T(8,128)} %fusion.2, bf16[2048,2048]{1,0:T(8,128)(2,1)} %all-gather.5.cloned.1.call-done, bf16[512,2048]{1,0:T(8,128)(2,1)} %get-tuple-element.26, bf16[2048]{0:T(1024)(128)(2,1)S(1)} %fusion.8), kind=kOutput, calls=%fused_computation.3 | convolution fusion | flops 4297064448 | bytes 18878464 | tf_op jit(solution)/shard_map/dot_general | solution.py:239
  263.5 72.2 %all-to-all-done.2 = bf16[32,4,128,128]{3,2,1,0:T(8,128)(2,1)} async-done(((bf16[32,4,128,128]{3,2,1,0:T(8,128)(2,1)}), bf16[32,4,128,128]{3,2,1,0:T(8,128)(2,1)}, u32[]{:S(2)}, u32[]{:S(2)}) %all-to-all-start.2) | async-done | bytes 4194336 | tf_op jit(solution)/shard_map/all_to_all | solution.py:206
  335.6 10.7 %finish.1 = f32[512,2048]{1,0:T(8,128)} custom-call(s32[32,4]{1,0:T(8,128)} %copy.24.idx, s32[1]{0:T(128)} %copy.25.width, s32[1]{0:T(128)S(6)} %sub.25.rows_left, bf16[128,128,128]{2,1,0:T(8,128)(2,1)} %bitcast.13.arrived, f32[512,2048]{1,0:T(8,128)} %convolution_subtract_fusion.direct), custom_call_target="tpu_custom_call" | custom-call | bytes 12582912 | tf_op jit(solution)/shard_map/finish/pallas_call | solution.py:179
  (14 shorter events, 0.1 us)
Async XLA Ops:
  6.5 235.9 %all-gather.3.cloned.1.call-start = ((), (), s32[]{:S(2)}) async-start(), calls=%async_computation.3 | async-start | bytes 10485760 | tf_op jit(solution)/shard_map/all_gather | solution.py:237
  125.3 4.6 %copy-start.3 = (s32[1,64,2]{1,2,0:T(2,128)S(1)}, s32[1,64,2]{1,2,0:T(2,128)}, u32[]{:S(2)}) copy-start(s32[1,64,2]{1,2,0:T(2,128)} %param.18) | copy-start | bytes 1540
  125.3 5.3 %copy-start.4 = (f32[1,64,2]{1,2,0:T(2,128)S(1)}, f32[1,64,2]{1,2,0:T(2,128)}, u32[]{:S(2)}) copy-start(f32[1,64,2]{1,2,0:T(2,128)} %param.19) | copy-start | bytes 1540
  125.3 6.6 %copy-start.5 = (s32[240]{0:T(256)S(1)}, s32[240]{0:T(256)}, u32[]{:S(2)}) copy-start(s32[240]{0:T(256)} %param.16) | copy-start | bytes 2884
  125.3 6.7 %copy-start.2 = (s32[1,2,1024]{2,1,0:T(2,128)S(1)}, s32[1,2,1024]{2,1,0:T(2,128)}, u32[]{:S(2)}) copy-start(s32[1,2,1024]{2,1,0:T(2,128)} %param.15) | copy-start | bytes 24580
  125.3 98.1 %all-to-all-start = ((bf16[32,4,128,128]{3,2,1,0:T(8,128)(2,1)}), bf16[32,4,128,128]{3,2,1,0:T(8,128)(2,1)}, u32[]{:S(2)}, u32[]{:S(2)}) async-start(bf16[32,4,128,128]{3,2,1,0:T(8,128)(2,1)} %bitcast.24), calls=%async_computation | async-start | bytes 8388608 | tf_op jit(solution)/shard_map/all_to_all | solution.py:206
  129.1 122.7 %all-gather.5.cloned.1.call-start = ((), (), s32[]{:S(2)}) async-start(), calls=%async_computation.4 | async-start | bytes 10485760 | tf_op jit(solution)/shard_map/all_gather | solution.py:236
  236.3 5.1 %copy-start.1 = (s32[1,2,2048]{2,1,0:T(2,128)S(1)}, s32[1,2,2048]{2,1,0:T(2,128)}, u32[]{:S(2)}) copy-start(s32[1,2,2048]{2,1,0:T(2,128)} %param.13) | copy-start | bytes 49156
  236.3 6.1 %copy-start = (bf16[512,2048]{1,0:T(8,128)(2,1)S(1)}, bf16[512,2048]{1,0:T(8,128)(2,1)}, u32[]{:S(2)}) copy-start(bf16[512,2048]{1,0:T(8,128)(2,1)} %get-tuple-element.24) | copy-start | bytes 6291460
  236.3 99.4 %all-to-all-start.2 = ((bf16[32,4,128,128]{3,2,1,0:T(8,128)(2,1)}), bf16[32,4,128,128]{3,2,1,0:T(8,128)(2,1)}, u32[]{:S(2)}, u32[]{:S(2)}) async-start(bf16[32,4,128,128]{3,2,1,0:T(8,128)(2,1)} %bitcast.25), calls=%async_computation.2 | async-start | bytes 8388608 | tf_op jit(solution)/shard_map/all_to_all | solution.py:206
Sparse Core Ops, SparseCore 0:
  24.4 101.6 all-gather.2
  131.5 92.2 all-gather.4

commit v2 on v1

v2 whole, which is shorter than its diff:
```python
import functools

import jax
import jax.numpy as jnp
from jax import lax
from jax.experimental import pallas as pl
from jax.experimental.pallas import tpu as pltpu
from jax.sharding import PartitionSpec as P

TILE = 128
F32 = jnp.float32
BF16 = jnp.bfloat16


def params(limit=60 << 20):
    return pltpu.CompilerParams(vmem_limit_bytes=limit)


def cost(moved, flops=0):
    return pl.CostEstimate(flops=flops, bytes_accessed=moved, transcendentals=0)


def select_kernel(
    row_tiles, steps, step_slots, cap, idx, width, rows_left, gen, ham, gen_b, ham_b, gen_out, ham_out, gen_tiles, ham_tiles
):
    i = pl.program_id(0)

    def cast(at, x_ref, b_ref, tiles):
        x = x_ref[...]
        rows = at * TILE + lax.broadcasted_iota(jnp.int32, x.shape, 0)
        cols = lax.broadcasted_iota(jnp.int32, x.shape, 1)
        v = jnp.where((rows < rows_left[0]) & (cols < width[0]), x, 0.0).astype(BF16)
        b_ref[...] = v
        col_tiles = x.shape[1] // TILE
        for c in range(col_tiles):
            tiles[at * col_tiles + c] = v[:, c * TILE : (c + 1) * TILE]

    def pick(at, out_ref, tiles):
        for k in range(step_slots):
            s = at * step_slots + k
            out_ref[k] = tiles[idx[s % cap, s // cap]]

    @pl.when(i < row_tiles)
    def _():
        cast(i, gen, gen_b, gen_tiles)

    @pl.when((i >= row_tiles) & (i < 2 * row_tiles))
    def _():
        cast(i - row_tiles, ham, ham_b, ham_tiles)

    @pl.when((i >= row_tiles) & (i < row_tiles + steps))
    def _():
        pick(i - row_tiles, gen_out, gen_tiles)

    @pl.when(i >= 2 * row_tiles)
    def _():
        pick(jnp.minimum(i - 2 * row_tiles, steps - 1), ham_out, ham_tiles)


def select_tiles(gen, ham, width, rows_left, slots):
    rows, cols = gen.shape
    cap, peers = slots.shape
    total = peers * cap
    row_tiles = rows // TILE
    steps = row_tiles
    step_slots = total // steps
    tiles = pltpu.VMEM((row_tiles * (cols // TILE), TILE, TILE), BF16)

    def window(first, count):
        return lambda i: jnp.clip(i - first, 0, count - 1)

    early, late = window(0, row_tiles), window(row_tiles, row_tiles)
    out_early, out_late = window(row_tiles, steps), window(2 * row_tiles, steps)
    slab = (TILE, cols)
    chunk = (step_slots, TILE, TILE)
    return pl.pallas_call(
        functools.partial(select_kernel, row_tiles, steps, step_slots, cap),
        grid_spec=pltpu.PrefetchScalarGridSpec(
            num_scalar_prefetch=3,
            grid=(2 * row_tiles + steps,),
            in_specs=[
                pl.BlockSpec(slab, lambda i, *_: (early(i), 0)),
                pl.BlockSpec(slab, lambda i, *_: (late(i), 0)),
            ],
            out_specs=(
                pl.BlockSpec(slab, lambda i, *_: (early(i), 0)),
                pl.BlockSpec(slab, lambda i, *_: (late(i), 0)),
                pl.BlockSpec(chunk, lambda i, *_: (out_early(i), 0, 0)),
                pl.BlockSpec(chunk, lambda i, *_: (out_late(i), 0, 0)),
            ),
            scratch_shapes=[tiles, tiles],
        ),
        out_shape=(jax.ShapeDtypeStruct((rows, cols), BF16),) * 2
        + (jax.ShapeDtypeStruct((total, TILE, TILE), BF16),) * 2,
        compiler_params=params(),
        cost_estimate=cost(12 * rows * cols + 4 * total * TILE * TILE),
        name="select_tiles",
    )(slots, width, rows_left, gen, ham)


def assemble_rows(i, side, src, coef, recv, dst, dst_w, w):
    for c in range(side):
        t = i * side + c
        one = recv[src[0, t]].astype(F32) * coef[0, t]
        two = recv[src[1, t]].astype(F32) * coef[1, t]
        tile = (one + two).astype(BF16)
        cols = slice(c * TILE, (c + 1) * TILE)
        rows = pl.ds(pl.multiple_of(i * TILE, TILE), TILE)
        dst[rows, cols] = tile
        dst_w[rows, cols] = tile * w[:, cols]


def commutator_kernel(side, src, coef, width, recv_gen, recv_ham, w, out_ref, ham_in, g, gw, h, hw, comm, sem):
    load = pltpu.make_async_copy(recv_ham, ham_in, sem)
    load.start()

    @pl.loop(0, side)
    def _(i):
        assemble_rows(i, side, src, coef, recv_gen, g, gw, w)

    load.wait()

    @pl.loop(0, side)
    def _(i):
        assemble_rows(i, side, src, coef, ham_in, h, hw, w)

    full = side * TILE
    step = 2 * TILE

    @pl.loop(0, full // step)
    def _(j):
        cols = pl.ds(pl.multiple_of(j * step, step), step)
        c = jnp.dot(gw[...], h[:, cols], preferred_element_type=F32)
        c = c - jnp.dot(hw[...], g[:, cols], preferred_element_type=F32)
        row = lax.broadcasted_iota(jnp.int32, (full, step), 0)
        col = j * step + lax.broadcasted_iota(jnp.int32, (full, step), 1)
        comm[:, cols] = jnp.where((row < width[0]) & (col < width[0]), c, 0.0).astype(BF16)

    @pl.loop(0, side)
    def _(i):
        rows = pl.ds(pl.multiple_of(i * TILE, TILE), TILE)
        for c in range(side):
            t = i * side + c
            tile = comm[rows, c * TILE : (c + 1) * TILE].astype(F32)
            out_ref[src[0, t]] = (tile * coef[0, t]).astype(BF16)
            out_ref[src[1, t]] = (tile * coef[1, t]).astype(BF16)


def commutator(recv_gen, recv_ham, src, coef, hole, w):
    full = w.shape[1]
    smem = pl.BlockSpec(memory_space=pltpu.SMEM)
    vmem = pl.BlockSpec(memory_space=pltpu.VMEM)
    return pl.pallas_call(
        functools.partial(commutator_kernel, full // TILE),
        in_specs=[smem, smem, smem, vmem, pl.BlockSpec(memory_space=pl.ANY), vmem],
        out_specs=vmem,
        out_shape=jax.ShapeDtypeStruct(recv_gen.shape, BF16),
        scratch_shapes=[pltpu.VMEM(recv_ham.shape, BF16)]
        + [pltpu.VMEM((full, full), BF16)] * 5
        + [pltpu.SemaphoreType.DMA],
        compiler_params=params(),
        cost_estimate=cost(6 * recv_gen.size, 4 * full * full * full),
        name="commutator",
    )(src, coef, hole, recv_gen, recv_ham, w)


def finish_kernel(steps, step_slots, cap, col_tiles, idx, width, rows_left, arrived, direct, out_ref, acc):
    i = pl.program_id(0)

    @pl.when(i == 0)
    def _():
        acc[...] = jnp.zeros_like(acc)

    @pl.when(i < steps)
    def _():
        for k in range(step_slots):
            s = i * step_slots + k
            j = idx[s % cap, s // cap]
            rows = pl.ds(pl.multiple_of(j // col_tiles * TILE, TILE), TILE)
            cols = pl.ds(pl.multiple_of(j % col_tiles * TILE, TILE), TILE)
            acc[rows, cols] += arrived[k].astype(F32)

    @pl.when(i >= steps)
    def _():
        base = (i - steps) * TILE
        v = acc[pl.ds(pl.multiple_of(base, TILE), TILE), :] + direct[...]
        rows = base + lax.broadcasted_iota(jnp.int32, v.shape, 0)
        cols = lax.broadcasted_iota(jnp.int32, v.shape, 1)
        out_ref[...] = jnp.where((rows < rows_left[0]) & (cols < width[0]), v, 0.0)


def finish(arrived, direct, width, rows_left, slots):
    rows, cols = direct.shape
    cap, peers = slots.shape
    step_slots = 16
    steps = peers * cap // step_slots
    return pl.pallas_call(
        functools.partial(finish_kernel, steps, step_slots, cap, cols // TILE),
        grid_spec=pltpu.PrefetchScalarGridSpec(
            num_scalar_prefetch=3,
            grid=(steps + rows // TILE,),
            in_specs=[
                pl.BlockSpec((step_slots, TILE, TILE), lambda i, *_: (jnp.minimum(i, steps - 1), 0, 0)),
                pl.BlockSpec((TILE, cols), lambda i, *_: (jnp.maximum(i - steps, 0), 0)),
            ],
            out_specs=pl.BlockSpec((TILE, cols), lambda i, *_: (jnp.maximum(i - steps, 0), 0)),
            scratch_shapes=[pltpu.VMEM((rows, cols), F32)],
        ),
        out_shape=jax.ShapeDtypeStruct((rows, cols), F32),
        compiler_params=params(),
        cost_estimate=cost(2 * arrived.size + 8 * rows * cols),
        name="finish",
    )(slots, width, rows_left, arrived, direct)


def occupancy(orbits, occupation):
    labels = jnp.arange(occupation.shape[0], dtype=jnp.int32)
    hit = (orbits[:, :, None] == labels) & (occupation == 1)
    return jnp.sum(hit.astype(F32), axis=2)


def forward_kernel(
    n_row, gen_in, ham_in, gen_b, ham_b, got_gen, got_ham, gen_rest, ham_rest, send, recv, ysend, yrecv, csend, crecv, local
):
    mesh_id = pl.DeviceIdType.MESH
    chan = lax.axis_index("chan")
    row = lax.axis_index("row")
    peers = gen_in.shape[0]
    me = chan * n_row + row
    group = peers // 4
    plane = me // group
    inner = lax.rem(me, group)
    n_y = n_row // 2
    y = row // 2
    core = lax.rem(row, 2)
    arrays = ((gen_in, got_gen), (ham_in, got_ham))
    slabs = ((gen_b, gen_rest), (ham_b, ham_rest))

    def place(p):
        return (p // n_row, lax.rem(p, n_row))

    barrier = pltpu.get_barrier_semaphore()

    @pl.loop(1, peers)
    def _(k):
        pl.semaphore_signal(barrier, inc=1, device_id=place(lax.rem(me + k, peers)), device_id_type=mesh_id)

    pl.semaphore_wait(barrier, peers - 1)

    def tile_copy(which, a, b):
        p = lax.rem(plane + a, 4) * group + lax.rem(inner + b, group)
        src, dst = arrays[which]
        k = a * group + b
        return pltpu.make_async_remote_copy(
            src_ref=src.at[p],
            dst_ref=dst.at[me],
            send_sem=send.at[which, k],
            recv_sem=recv.at[which, k],
            device_id=place(p),
            device_id_type=mesh_id,
        )

    def slab_copy(which, dy):
        src, dst = slabs[which]
        return pltpu.make_async_remote_copy(
            src_ref=src,
            dst_ref=dst.at[2 * dy - 1],
            send_sem=ysend.at[which, dy],
            recv_sem=yrecv.at[which, dy],
            device_id=(chan, lax.rem(y + dy, n_y) * 2 + core),
            device_id_type=mesh_id,
        )

    def core_copy(which, dy):
        src, dst = slabs[which]
        return pltpu.make_async_remote_copy(
            src_ref=src if dy == 0 else dst.at[2 * dy - 1],
            dst_ref=dst.at[2 * dy],
            send_sem=csend.at[which, dy],
            recv_sem=crecv.at[which, dy],
            device_id=(chan, y * 2 + 1 - core),
            device_id_type=mesh_id,
        )

    own = [pltpu.make_async_copy(arrays[w][0].at[me], arrays[w][1].at[me], local.at[w]) for w in range(2)]
    for w in range(2):
        own[w].start()
        core_copy(w, 0).start()
    turn = plane * plane // 4

    @pl.loop(0, 3)
    def _(i):
        a = 1 + lax.rem(i + turn, 3)

        @pl.loop(0, group)
        def _(b):
            tile_copy(0, a, b).start()
            tile_copy(1, a, b).start()

    for dy in range(1, n_y):
        for w in range(2):
            slab_copy(w, dy).start()

    @pl.loop(1, group)
    def _(b):
        tile_copy(0, 0, b).start()
        tile_copy(1, 0, b).start()

    for dy in range(1, n_y):
        for w in range(2):
            slab_copy(w, dy).wait()
            core_copy(w, dy).start()

    @pl.loop(1, peers)
    def _(k):
        for w in range(2):
            tile_copy(w, k // group, lax.rem(k, group)).wait()

    for w in range(2):
        own[w].wait()
        for dy in range(n_y):
            core_copy(w, dy).wait()


def forward(gen_out, ham_out, gen_b, ham_b, peers, n_row):
    shape = (peers, gen_out.shape[0] // peers) + gen_out.shape[1:]
    rest = (n_row - 1,) + gen_b.shape
    hbm = pl.BlockSpec(memory_space=pl.ANY)
    dma = pltpu.SemaphoreType.DMA
    got_gen, got_ham, gen_rest, ham_rest = pl.pallas_call(
        functools.partial(forward_kernel, n_row),
        in_specs=[hbm] * 4,
        out_specs=(hbm,) * 4,
        out_shape=(jax.ShapeDtypeStruct(shape, BF16),) * 2 + (jax.ShapeDtypeStruct(rest, BF16),) * 2,
        scratch_shapes=[
            dma((2, peers)),
            dma((2, peers)),
            dma((2, n_row)),
            dma((2, n_row)),
            dma((2, n_row)),
            dma((2, n_row)),
            dma((2,)),
        ],
        compiler_params=pltpu.CompilerParams(
            collective_id=0, has_side_effects=True, vmem_limit_bytes=60 << 20
        ),
        cost_estimate=cost(8 * gen_out.size),
        name="forward",
    )(gen_out.reshape(shape), ham_out.reshape(shape), gen_b, ham_b)
    return got_gen.reshape(gen_out.shape), got_ham.reshape(ham_out.shape), gen_rest, ham_rest


def ordered(left, order, rows):
    return jnp.concatenate([lax.dynamic_slice_in_dim(left, o * rows, rows, axis=1) for o in order], axis=1)


def exchange(tiles, peers):
    shaped = tiles.reshape((peers, -1) + tiles.shape[1:])
    moved = lax.all_to_all(shaped, ("chan", "row"), split_axis=0, concat_axis=0, tiled=True)
    return moved.reshape(tiles.shape)


def on_device(
    generator, hamiltonian, pp_width, pp_orbit, ph_width, ph_orbit, occupation, send_tile, ph_source, ph_coef
):
    slab_rows = generator.shape[1]
    full_width = generator.shape[2]
    hole_width = ph_orbit.shape[2]
    slots = send_tile[0].T
    src = ph_source[0].T
    coef = ph_coef[0].T
    peers = slots.shape[1]
    rows_left = pp_width - lax.axis_index("row") * slab_rows

    gen_b, ham_b, gen_out, ham_out = select_tiles(generator[0], hamiltonian[0], pp_width, rows_left, slots)
    n_row = full_width // slab_rows
    got_gen, got_ham, gen_rest, ham_rest = forward(gen_out, ham_out, gen_b, ham_b, peers, n_row)

    col_ok = jnp.arange(full_width, dtype=jnp.int32) < pp_width[0]
    pair = occupancy(pp_orbit[0], occupation)
    weight_pp = jnp.where(col_ok, 1.0 - pair[0] - pair[1], 0.0).astype(BF16)
    hole_cols = jnp.arange(hole_width, dtype=jnp.int32) < ph_width[0]
    hole = occupancy(ph_orbit[0], occupation)
    weight_ph = jnp.where(hole_cols, hole[0] - hole[1], 0.0).astype(BF16)[None]

    row = lax.axis_index("row")
    y, core = row // 2, row % 2
    order = []
    for dy in range(n_row // 2):
        other = (y + n_row // 2 - dy) % (n_row // 2)
        order += [other * 2 + core, other * 2 + 1 - core]
    gen_all = jnp.concatenate([gen_b, gen_rest.reshape(-1, full_width)])
    ham_all = jnp.concatenate([ham_b, ham_rest.reshape(-1, full_width)])
    first = jnp.dot(ordered(gen_b * weight_pp[None, :], order, slab_rows), ham_all, preferred_element_type=F32)
    second = jnp.dot(ordered(ham_b * weight_pp[None, :], order, slab_rows), gen_all, preferred_element_type=F32)
    direct = first - second

    returned = commutator(got_gen, got_ham, src, coef, ph_width, weight_ph)
    arrived = exchange(returned, peers)
    return finish(arrived, direct, pp_width, rows_left, slots)[None]


def solution(mesh):
    in_specs = (
        P("chan", "row", None),
        P("chan", "row", None),
        P("chan"),
        P("chan", None, None),
        P(("chan", "row")),
        P(("chan", "row"), None, None),
        P(),
        P(("chan", "row"), None, None),
        P(("chan", "row"), None, None),
        P(("chan", "row"), None, None),
    )
    out_specs = P("chan", "row", None)
    return jax.shard_map(
        on_device, mesh=mesh, in_specs=in_specs, out_specs=out_specs, check_vma=False
    )
```

time: 354 us -> 350 us (0.989)
  Pallas kernels: 44.8 us -> 228 us
  blocking collectives: 101 us -> 0 us
  waiting for transfers between devices: 158 us -> 75.4 us
  starting transfers between devices: 8.98 us -> 22.9 us
  between operations: 14.8 us -> 1.5 us
  matrix products: 21.1 us -> 14.1 us
    pallas_call x3 -> x2, Pallas kernels: 21.2 us -> 203 us  [the longest x1 190 us: forward(): pl.pallas_call(functools.partial(forward_kernel, n_row), in_specs=[hbm] *...]
    all_to_all x1 -> x0, blocking collectives: 101 us -> none  [exchange(): lax.all_to_all(shaped, ('chan', 'row'), split_axis=0, concat_axis=0, tile...]
    all_to_all x2 -> x1, waiting for transfers between devices: 157 us -> 75.4 us  [exchange(): lax.all_to_all(shaped, ('chan', 'row'), split_axis=0, concat_axis=0, tile...]
    all_to_all x2 -> x1, starting transfers between devices: 8.93 us -> 22.9 us  [exchange(): lax.all_to_all(shaped, ('chan', 'row'), split_axis=0, concat_axis=0, tile...]
    dot_general x2, matrix products: 21.1 us -> 14.1 us  [the longest x1 7.63 us: on_device(): jnp.dot(ordered(gen_b * weight_pp[None, :], order, slab_rows), ham_all, p...]
  transfers between devices with their start and end apart: 4 -> 1, of which waited for: 2 -> 1; matrix products, arithmetic and copies ran while one was open for 7% -> 5% of each run, Pallas kernels for 5% -> 0%
where the time goes in v2:
time: 350 us; the launch traced here: 349 us
  Pallas kernels  228 us (65%)
  waiting for transfers between devices  75.4 us (22%)
  starting transfers between devices  22.9 us (7%)
  matrix products  14.1 us (4%)
  other arithmetic  5.17 us (1%)
    pallas_call x1, Pallas kernels, forward(): pl.pallas_call(functools.partial(forward_kernel, n_row), in_specs=[hbm] *...  190 us
    all_to_all x1, waiting for transfers between devices, exchange(): lax.all_to_all(shaped, ('chan', 'row'), split_axis=0, concat_axis=0, tile...  75.4 us
    all_to_all x1, starting transfers between devices, exchange(): lax.all_to_all(shaped, ('chan', 'row'), split_axis=0, concat_axis=0, tile...  22.9 us
    pallas_call x1, Pallas kernels, commutator(): pl.pallas_call(functools.partial(commutator_kernel, full // TILE), in_spe...  13.8 us
    pallas_call x1, Pallas kernels, select_tiles(): pl.pallas_call(functools.partial(select_kernel, row_tiles, steps, step_sl...  12.4 us
    pallas_call x1, Pallas kernels, finish(): pl.pallas_call(functools.partial(finish_kernel, steps, step_slots, cap, c...  11.8 us
    dot_general x1, matrix products, on_device(): jnp.dot(ordered(gen_b * weight_pp[None, :], order, slab_rows), ham_all, p...  7.63 us
  transfers between devices with their start and end apart: 1, of which 1 were waited for; matrix products, arithmetic and copies ran while one was open for 5% of the time, Pallas kernels for 0%

profile of v2, /device:TPU:0, one launch (start us, length us, event | category | flops | bytes accessed | tf_op | source)
XLA Modules:
  0.0 348.9 jit_solution(6712718816348661677)
XLA Ops:
  1.3 0.7 broadcast_compare_fusion
  2.0 1.1 convert_reduce_fusion.1
  3.1 0.6 fusion.29.w
  3.7 12.4 %select_tiles.1 = (bf16[512,2048]{1,0:T(8,128)(2,1)}, bf16[512,2048]{1,0:T(8,128)(2,1)}, bf16[128,128,128]{2,1,0:T(8,128)(2,1)}, bf16[128,128,128]{2,1,0:T(8,128)(2,1)}) custom-call(s32[4,32]{1,0:T(4,128)} %bitcast.34, s32[1]{0:T(128)} %copy.11.width, s32[1]{0:T(128)S(6)} %sub.38.rows_left, f32[512,2048]{1,0:T(8,128)} %bitcast.29, f32[512,2048]{1,0:T(8,128)} %bitcast.30), custom_call_target="tpu_custom_call" | custom-call | bytes 20971520 | tf_op jit(solution)/shard_map/select_tiles/pallas_call | solution.py:76
  16.1 190.2 %forward.1 = (bf16[32,4,128,128]{3,2,1,0:T(8,128)(2,1)}, bf16[32,4,128,128]{3,2,1,0:T(8,128)(2,1)}, bf16[3,512,2048]{2,1,0:T(8,128)(2,1)}, bf16[3,512,2048]{2,1,0:T(8,128)(2,1)}) custom-call(bf16[32,4,128,128]{3,2,1,0:T(8,128)(2,1)} %bitcast.27, bf16[32,4,128,128]{3,2,1,0:T(8,128)(2,1)} %bitcast.28, bf16[512,2048]{1,0:T(8,128)(2,1)} %get-tuple-element.15.gen_b, ...), custom_call_target="tpu_custom_call" | custom-call | bytes 16777216 | tf_op jit(solution)/shard_map/forward/pallas_call | solution.py:330
  206.3 13.8 %commutator.1 = bf16[128,128,128]{2,1,0:T(8,128)(2,1)} custom-call(s32[2,64]{1,0:T(2,128)} %bitcast.42, f32[2,64]{1,0:T(2,128)} %bitcast.43, s32[1]{0:T(128)} %copy.12.width, bf16[128,128,128]{2,1,0:T(8,128)(2,1)} %bitcast.40, bf16[128,128,128]{2,1,0:T(8,128)(2,1)} %bitcast.41, bf16[1,1024]{1,0:T(2,128)(2,1)} %fusion.29.w), custom_call_target="tpu_custom_call" | custom-call | flops 4294967296 | bytes 12582912 | tf_op jit(solution)/shard_map/commutator/pallas_call | solution.py:153
  220.1 0.0 copy-start.2
  220.1 0.0 copy-start
  220.1 22.9 %all-to-all-start = ((bf16[32,4,128,128]{3,2,1,0:T(8,128)(2,1)}), bf16[32,4,128,128]{3,2,1,0:T(8,128)(2,1)}, u32[]{:S(2)}, u32[]{:S(2)}) async-start(bf16[32,4,128,128]{3,2,1,0:T(8,128)(2,1)} %bitcast.31), calls=%async_computation | async-start | bytes 8388608 | tf_op jit(solution)/shard_map/all_to_all | solution.py:359
  243.1 0.0 copy-done.2
  243.1 0.9 convert_reduce_fusion
  244.1 0.0 copy-done
  244.1 1.9 broadcast_multiply_fusion
  245.9 0.0 copy-start.1
  246.0 0.0 slice-start
  246.0 0.5 constant_dynamic-slice_fusion.3
  246.5 1.0 copy-done.1
  247.5 0.0 slice-start.1
  247.5 7.6 %fusion = f32[512,2048]{1,0:T(8,128)S(1)} fusion(bf16[1536,2048]{1,0:T(8,128)(2,1)} %bitcast.39, bf16[512,2048]{1,0:T(8,128)(2,1)S(1)} %copy-done.1, bf16[512,512]{1,0:T(8,128)(2,1)S(1)} %get-tuple-element.33, bf16[512,512]{1,0:T(8,128)(2,1)S(1)} %get-tuple-element.32, bf16[512,512]{1,0:T(8,128)(2,1)S(1)} %get-tuple-element.31, ...), kind=kOutput, calls=%fused_computation | convolution fusion | flops 4320133120 | bytes 14680064 | tf_op jit(solution)/shard_map/dot_general | solution.py:394
  255.2 0.0 slice-done
  255.2 0.0 slice-done.1
  255.2 6.5 %fusion.9.direct = f32[512,2048]{1,0:T(8,128)} fusion(f32[512,2048]{1,0:T(8,128)S(1)} %fusion, bf16[1536,2048]{1,0:T(8,128)(2,1)S(1)} %bitcast.38, bf16[512,2048]{1,0:T(8,128)(2,1)S(1)} %copy-done, bf16[512,512]{1,0:T(8,128)(2,1)S(1)} %get-tuple-element.22, bf16[512,512]{1,0:T(8,128)(2,1)S(1)} %get-tuple-element.23, ...), kind=kOutput, calls=%fused_computation.11 | convolution fusion | flops 4321181696 | bytes 18874368 | tf_op jit(solution)/shard_map/dot_general | solution.py:395
  261.7 75.4 %all-to-all-done = bf16[32,4,128,128]{3,2,1,0:T(8,128)(2,1)} async-done(((bf16[32,4,128,128]{3,2,1,0:T(8,128)(2,1)}), bf16[32,4,128,128]{3,2,1,0:T(8,128)(2,1)}, u32[]{:S(2)}, u32[]{:S(2)}) %all-to-all-start) | async-done | bytes 4194336 | tf_op jit(solution)/shard_map/all_to_all | solution.py:359
  337.1 11.8 %finish.1 = f32[512,2048]{1,0:T(8,128)} custom-call(s32[4,32]{1,0:T(4,128)} %bitcast.35, s32[1]{0:T(128)} %copy.11.width, s32[1]{0:T(128)S(6)} %sub.38.rows_left, bf16[128,128,128]{2,1,0:T(8,128)(2,1)} %bitcast.17.arrived, f32[512,2048]{1,0:T(8,128)} %fusion.9.direct), custom_call_target="tpu_custom_call" | custom-call | bytes 12582912 | tf_op jit(solution)/shard_map/finish/pallas_call | solution.py:197
  (2 shorter events, 0.0 us)
Async XLA Ops:
  220.1 23.0 %copy-start.2 = (s32[1,2,2048]{2,1,0:T(2,128)S(1)}, s32[1,2,2048]{2,1,0:T(2,128)}, u32[]{:S(2)}) copy-start(s32[1,2,2048]{2,1,0:T(2,128)} %param.13) | copy-start | bytes 49156
  220.1 24.0 %copy-start = (bf16[512,2048]{1,0:T(8,128)(2,1)S(1)}, bf16[512,2048]{1,0:T(8,128)(2,1)}, u32[]{:S(2)}) copy-start(bf16[512,2048]{1,0:T(8,128)(2,1)} %get-tuple-element.15.gen_b) | copy-start | bytes 6291460
  220.1 117.0 %all-to-all-start = ((bf16[32,4,128,128]{3,2,1,0:T(8,128)(2,1)}), bf16[32,4,128,128]{3,2,1,0:T(8,128)(2,1)}, u32[]{:S(2)}, u32[]{:S(2)}) async-start(bf16[32,4,128,128]{3,2,1,0:T(8,128)(2,1)} %bitcast.31), calls=%async_computation | async-start | bytes 8388608 | tf_op jit(solution)/shard_map/all_to_all | solution.py:359
  245.9 1.6 copy-start.1
  246.0 9.2 %slice-start = ((s8[6291456]{0:T(1024)(128)(4,1)}), s8[4194304]{0:T(1024)(128)(4,1)S(1)}, s32[]{:S(2)}) async-start(s8[6291456]{0:T(1024)(128)(4,1)} %bitcast.36), calls=%async_computation.1 | async-start | bytes 8388608
  247.5 7.6 %slice-start.1 = ((s8[6291456]{0:T(1024)(128)(4,1)}), s8[2097152]{0:T(1024)(128)(4,1)S(1)}, s32[]{:S(2)}) async-start(s8[6291456]{0:T(1024)(128)(4,1)} %bitcast.36), calls=%async_computation.2 | async-start | bytes 4194304
